TPU v7x, 256 devices: a whole 4x4x8 slice. The times are simulated.
256 devices in a mesh: gy: 64 (over x, y, z_hi, core), gz: 4 (over z_lo).
Axes of the slice: x: 4, y: 4, z: 8 (z_hi: 2, z_lo: 4; z = z_hi * 4 + z_lo), core: 2. Of those that a mesh axis runs over, the one named last changes fastest.
Arguments:
- efield_check: bfloat16 [3, 2048, 8, 1024], P(None, 'gy', None, 'gz'), may hold values from -6 to 6
- hfield_check: bfloat16 [3, 2048, 8, 1024], P(None, 'gy', None, 'gz'), may hold values from -6 to 6
- polar_check: bfloat16 [3, 2048, 8, 1024], P(None, 'gy', None, 'gz'), may hold values from -4 to 4
- rate_check: bfloat16 [3, 2048, 8, 1024], P(None, 'gy', None, 'gz'), may hold values from -4 to 4
- levels_check: bfloat16 [2, 2048, 8, 1024], P(None, 'gy', None, 'gz'), may hold values from 0.049804688 to 0.5
- efield_seed: float32 [3, 2048, 8, 1024], P(None, 'gy', None, 'gz'), may hold values from -6 to 6
- hfield_seed: float32 [3, 2048, 8, 1024], P(None, 'gy', None, 'gz'), may hold values from -6 to 6
- polar_seed: float32 [3, 2048, 8, 1024], P(None, 'gy', None, 'gz'), may hold values from -6 to 6
- rate_seed: float32 [3, 2048, 8, 1024], P(None, 'gy', None, 'gz'), may hold values from -6 to 6
- levels_seed: float32 [2, 2048, 8, 1024], P(None, 'gy', None, 'gz'), may hold values from -6 to 6
- material_labels: int32 [2048, 8, 1024], P('gy', None, 'gz'), may hold values from 0 to 3
- gain_labels: int32 [2048, 8, 1024], P('gy', None, 'gz'), may hold values 0 or 1
- inverse_table: float32 [4], replicated, may hold values from 0.08 to 1
- source_field: float32 [2048, 8, 1024], P('gy', None, 'gz'), may hold values from -6 to 6
- start_step: int32 [1], replicated, may hold values from 0 to 255
Outputs:
- efield_grad: float32 [3, 2048, 8, 1024], P(None, 'gy', None, 'gz')
- hfield_grad: float32 [3, 2048, 8, 1024], P(None, 'gy', None, 'gz')
- polar_grad: float32 [3, 2048, 8, 1024], P(None, 'gy', None, 'gz')
- rate_grad: float32 [3, 2048, 8, 1024], P(None, 'gy', None, 'gz')
- levels_grad: float32 [2, 2048, 8, 1024], P(None, 'gy', None, 'gz')
- cell_grad: float32 [2048, 8, 1024], P('gy', None, 'gz')
- table_grad: float32 [4], replicated
All inputs are finite; a program needn't handle non-finite values. No bound on the sum of `gain_labels` on one device may be relied on, other than what follows from the above.
Results may differ from a plain program's by a relative error of at most 0.0003.
Values may be sent and summed in bfloat16 or wider, within the bound.
No kernel may reach another device: no remote copies, remote signals or barrier semaphores. Data moves between devices by JAX's collectives and lax.ppermute only.
A program may use at most 64 MiB of HBM per device.

v0:
```python
import math
import jax
import jax.numpy as jnp
from jax import lax
from jax.sharding import PartitionSpec as P

MAGNETIC_STEP = 0.5
ELECTRIC_STEP = 0.5
TIME_STEP = 0.5
DAMPING = 0.9
STIFFNESS = 0.3
COUPLING = 0.4
PUMPING = 0.05
UPPER_DECAY = 0.02
LOWER_DECAY = 0.3
STIMULATED = 0.2
SOURCE_OMEGA = 0.35


def shifted(block, axis, distance):
    devices = range(lax.axis_size(axis))
    route = [(i - distance, i) for i in devices if i - distance in devices]
    return lax.ppermute(block, axis, route)


def front(values, axis):
    rest = lax.slice_in_dim(values, 1, values.shape[axis], axis=axis)
    border = jnp.zeros_like(lax.slice_in_dim(values, 0, 1, axis=axis))
    return jnp.concatenate([rest, border], axis)


def behind(values, axis):
    rest = lax.slice_in_dim(values, 0, values.shape[axis] - 1, axis=axis)
    border = jnp.zeros_like(lax.slice_in_dim(values, 0, 1, axis=axis))
    return jnp.concatenate([border, rest], axis)


def curl_from(along_x, along_y, along_z):
    return jnp.stack([along_y[2] - along_z[1], along_z[0] - along_x[2], along_x[1] - along_y[0]])


def curl_forward(field):
    front_row = shifted(field[:, :1], "gy", -1)
    front_column = shifted(field[:, :, :, :1], "gz", -1)
    along_y = jnp.concatenate([field[:, 1:], front_row], 1) - field
    along_z = jnp.concatenate([field[:, :, :, 1:], front_column], 3) - field
    along_x = front(field, 2) - field
    return curl_from(along_x, along_y, along_z)


def curl_backward(field):
    back_row = shifted(field[:, -1:], "gy", 1)
    back_column = shifted(field[:, :, :, -1:], "gz", 1)
    along_y = field - jnp.concatenate([back_row, field[:, :-1]], 1)
    along_z = field - jnp.concatenate([back_column, field[:, :, :, :-1]], 3)
    along_x = field - behind(field, 2)
    return curl_from(along_x, along_y, along_z)


def local_update(
    efield, polar_field, polar_rate, levels, curl_field, inverse, gain_region, source_push
):
    rate_next = (
        DAMPING * polar_rate
        - STIFFNESS * polar_field
        + COUPLING * gain_region * (levels[0] - levels[1]) * efield
    )
    polar_next = polar_field + TIME_STEP * rate_next
    forcing = ELECTRIC_STEP * curl_field - (polar_next - polar_field)
    forcing = jnp.concatenate([forcing[:2], forcing[2:] - source_push[None]], 0)
    efield_next = efield + inverse * forcing
    stimulated = STIMULATED * gain_region * jnp.sum(efield_next * rate_next, axis=0)
    upper = (
        levels[0]
        + TIME_STEP * (PUMPING * (1.0 - levels[0] - levels[1]) - UPPER_DECAY * levels[0])
        - stimulated
    )
    lower = levels[1] + TIME_STEP * (UPPER_DECAY * levels[0] - LOWER_DECAY * levels[1]) + stimulated
    return (efield_next, polar_next, rate_next, jnp.stack([upper, lower]))


def reverse_local(
    efield, polar_field, polar_rate, levels, curl_field, inverse, gain_region, source_push, seeds
):

    def update(first, second, third, fourth, fifth, sixth):
        return local_update(first, second, third, fourth, fifth, sixth, gain_region, source_push)

    unused, pullback = jax.vjp(update, efield, polar_field, polar_rate, levels, curl_field, inverse)
    return pullback(seeds)


def material_map(material_labels, inverse_table):
    inverse = jnp.zeros(material_labels.shape, jnp.float32)
    for label in range(inverse_table.shape[0]):
        inverse = inverse + jnp.where(
            material_labels == label, inverse_table[label], jnp.float32(0.0)
        )
    return inverse


def label_sums(material_labels, values, count):
    return jnp.stack(
        [
            jnp.sum(jnp.where(material_labels == label, values, jnp.float32(0.0)))
            for label in range(count)
        ]
    )


def step_total(material_labels, values, count):
    return lax.psum(label_sums(material_labels, values, count), ("gy", "gz"))


def on_device(
    efield_check,
    hfield_check,
    polar_check,
    rate_check,
    levels_check,
    efield_seed,
    hfield_seed,
    polar_seed,
    rate_seed,
    levels_seed,
    material_labels,
    gain_labels,
    inverse_table,
    source_field,
    start_step,
):
    count = inverse_table.shape[0]
    inverse = material_map(material_labels, inverse_table)
    gain_region = gain_labels.astype(jnp.float32)
    start = start_step[0].astype(jnp.float32)
    first_sine = jnp.sin(SOURCE_OMEGA * start)
    push_first = first_sine * source_field
    push_second = jnp.sin(SOURCE_OMEGA * (start + 1.0)) * source_field
    efield = efield_check.astype(jnp.float32)
    polar_field = polar_check.astype(jnp.float32)
    polar_rate = rate_check.astype(jnp.float32)
    levels = levels_check.astype(jnp.float32)
    hfield = hfield_check.astype(jnp.float32)
    hfield_mid = hfield - MAGNETIC_STEP * curl_forward(efield)
    curl_first = curl_backward(hfield_mid)
    state_one = local_update(
        efield, polar_field, polar_rate, levels, curl_first, inverse, gain_region, push_first
    )
    hfield_next = hfield_mid - MAGNETIC_STEP * curl_forward(state_one[0])
    curl_second = curl_backward(hfield_next)
    back_e, back_p, back_q, back_n, back_c, grad_second = reverse_local(
        state_one[0],
        state_one[1],
        state_one[2],
        state_one[3],
        curl_second,
        inverse,
        gain_region,
        push_second,
        (efield_seed, polar_seed, rate_seed, levels_seed),
    )
    h_back = hfield_seed + curl_forward(back_c)
    e_back = back_e - MAGNETIC_STEP * curl_backward(h_back)
    last_e, polar_grad, rate_grad, levels_grad, last_c, grad_first = reverse_local(
        efield,
        polar_field,
        polar_rate,
        levels,
        curl_first,
        inverse,
        gain_region,
        push_first,
        (e_back, back_p, back_q, back_n),
    )
    hfield_grad = h_back + curl_forward(last_c)
    efield_grad = last_e - MAGNETIC_STEP * curl_backward(hfield_grad)
    cell_grad = grad_second + grad_first
    cells = (
        material_labels.shape[0]
        * material_labels.shape[1]
        * material_labels.shape[2]
        * lax.axis_size("gy")
        * lax.axis_size("gz")
    )
    totals = step_total(material_labels, grad_second, count) + step_total(
        material_labels, grad_first, count
    )
    table_grad = totals * (1.0 / math.sqrt(cells))
    return (efield_grad, hfield_grad, polar_grad, rate_grad, levels_grad, cell_grad, table_grad)


def solution(mesh):
    placed = (
        P(None, "gy", None, "gz"),
        P(None, "gy", None, "gz"),
        P(None, "gy", None, "gz"),
        P(None, "gy", None, "gz"),
        P(None, "gy", None, "gz"),
        P(None, "gy", None, "gz"),
        P(None, "gy", None, "gz"),
        P(None, "gy", None, "gz"),
        P(None, "gy", None, "gz"),
        P(None, "gy", None, "gz"),
        P("gy", None, "gz"),
        P("gy", None, "gz"),
        P(),
        P("gy", None, "gz"),
        P(),
    )
    return jax.shard_map(
        on_device,
        mesh=mesh,
        in_specs=placed,
        out_specs=(
            P(None, "gy", None, "gz"),
            P(None, "gy", None, "gz"),
            P(None, "gy", None, "gz"),
            P(None, "gy", None, "gz"),
            P(None, "gy", None, "gz"),
            P("gy", None, "gz"),
            P(),
        ),
        check_vma=False,
    )
```

profile of v0, /device:TPU:2, one launch (start us, length us, event | category | flops | bytes accessed | tf_op | source)
XLA Modules:
  0.0 215.5 jit_solution(16821565105719444470)
XLA Ops:
  0.6 1.0 slice.413
  1.7 1.3 collective-permute-start.1
  3.0 11.0 %collective-permute-start = (f32[3,1,8,256]{3,2,1,0:T(8,128)S(1)}, f32[3,1,8,256]{3,2,1,0:T(8,128)S(1)}, u32[]{:S(2)}, u32[]{:S(2)}) collective-permute-start(f32[3,1,8,256]{3,2,1,0:T(8,128)S(1)} %slice.410), channel_id=1, source_target_pairs={{4,0},{8,4},{12,8},{16,12},{20,16},{24,20},{28,24},{32,28},{36,32}... | collective-permute-start | bytes 73736 | tf_op jit(solution)/shard_map/ppermute | solution.py:23
  14.0 0.6 fusion.15
  14.9 0.9 copy-done.18
  15.9 0.3 convert_subtract_fusion.2
  16.2 0.9 copy-done.14
  17.4 4.3 %collective-permute-start.3 = (f32[3,32,8,1]{3,2,1,0:T(8,128)S(1)}, f32[3,32,8,1]{3,2,1,0:T(8,128)S(1)}, u32[]{:S(2)}, u32[]{:S(2)}) collective-permute-start(f32[3,32,8,1]{3,2,1,0:T(8,128)S(1)} %slice.423), channel_id=1, source_target_pairs={{0,1},{1,2},{2,3},{4,5},{5,6},{6,7},{8,9},{9,10},{10,11},{12,13},{... | collective-permute-start | bytes 9224 | tf_op jit(solution)/shard_map/ppermute | solution.py:23
  21.7 5.1 %collective-permute-start.2 = (f32[3,1,8,256]{3,2,1,0:T(8,128)S(1)}, f32[3,1,8,256]{3,2,1,0:T(8,128)S(1)}, u32[]{:S(2)}, u32[]{:S(2)}) collective-permute-start(f32[3,1,8,256]{3,2,1,0:T(8,128)S(1)} %slice.420), channel_id=1, source_target_pairs={{0,4},{4,8},{8,12},{12,16},{16,20},{20,24},{24,28},{28,32},{32,36}... | collective-permute-start | bytes 73736 | tf_op jit(solution)/shard_map/ppermute | solution.py:23
  26.8 2.8 %select_add_fusion.2 = (f32[32,8,256]{2,1,0:T(8,128)S(1)}, pred[32,8,256]{2,1,0:T(8,128)(4,1)S(1)}, pred[32,8,256]{2,1,0:T(8,128)(4,1)S(1)}, pred[32,8,256]{2,1,...) fusion(f32[]{:T(128)} %bitcast.6, f32[]{:T(128)} %bitcast.5, f32[]{:T(128)} %bitcast.4, ...), kind=kLoop, calls=%fused_computation.118 | loop fusion | flops 983040 | bytes 1835024 | tf_op jit(solution)/shard_map/add | solution.py:96
  30.5 8.8 %collective-permute-done.2 = f32[3,1,8,256]{3,2,1,0:T(8,128)S(1)} collective-permute-done((f32[3,1,8,256]{3,2,1,0:T(8,128)S(1)}, f32[3,1,8,256]{3,2,1,0:T(8,128)S(1)}, u32[]{:S(2)}, u32[]{:S(2)}) %collective-permute-start.2) | collective-permute-done | bytes 24608 | tf_op jit(solution)/shard_map/ppermute | solution.py:23
  39.2 0.4 maximum_subtract_fusion.1
  39.8 0.9 copy-done.3
  40.8 0.3 fusion.3
  41.2 0.9 copy-done.15
  42.1 0.3 multiply_reduce_fusion.3
  42.5 1.4 collective-permute-start.5
  43.9 1.9 collective-permute-start.4
  46.0 0.3 slice.436
  46.5 5.8 %collective-permute-done.5 = f32[3,32,8,1]{3,2,1,0:T(8,128)S(1)} collective-permute-done((f32[3,32,8,1]{3,2,1,0:T(8,128)S(1)}, f32[3,32,8,1]{3,2,1,0:T(8,128)S(1)}, u32[]{:S(2)}, u32[]{:S(2)}) %collective-permute-start.5) | collective-permute-done | bytes 3104 | tf_op jit(solution)/shard_map/ppermute | solution.py:23
  52.3 0.3 maximum_subtract_fusion.3
  53.0 2.0 collective-permute-start.7
  55.0 1.9 collective-permute-start.6
  57.2 5.5 %collective-permute-done.7 = f32[3,32,8,1]{3,2,1,0:T(8,128)S(1)} collective-permute-done((f32[3,32,8,1]{3,2,1,0:T(8,128)S(1)}, f32[3,32,8,1]{3,2,1,0:T(8,128)S(1)}, u32[]{:S(2)}, u32[]{:S(2)}) %collective-permute-start.7) | collective-permute-done | bytes 3104 | tf_op jit(solution)/shard_map/ppermute | solution.py:23
  62.8 7.7 %collective-permute-done.6 = f32[3,1,8,256]{3,2,1,0:T(8,128)S(1)} collective-permute-done((f32[3,1,8,256]{3,2,1,0:T(8,128)S(1)}, f32[3,1,8,256]{3,2,1,0:T(8,128)S(1)}, u32[]{:S(2)}, u32[]{:S(2)}) %collective-permute-start.6) | collective-permute-done | bytes 24608 | tf_op jit(solution)/shard_map/ppermute | solution.py:23
  70.5 0.4 maximum_subtract_fusion.5
  71.0 0.5 fusion.4
  71.7 1.0 copy-done.16
  72.7 0.5 multiply_reduce_fusion.1
  73.3 1.0 copy-done.6
  74.3 0.2 copy-done.17
  74.6 0.5 multiply_reduce_fusion.2
  75.1 1.3 collective-permute-start.9
  76.4 1.9 collective-permute-start.8
  78.4 0.6 copy-done.22
  79.4 0.3 slice.460
  79.8 5.0 %collective-permute-done.9 = f32[3,32,8,1]{3,2,1,0:T(8,128)S(1)} collective-permute-done((f32[3,32,8,1]{3,2,1,0:T(8,128)S(1)}, f32[3,32,8,1]{3,2,1,0:T(8,128)S(1)}, u32[]{:S(2)}, u32[]{:S(2)}) %collective-permute-start.9) | collective-permute-done | bytes 3104 | tf_op jit(solution)/shard_map/ppermute | solution.py:23
  84.8 0.3 maximum_subtract_fusion.7
  85.3 1.1 copy-done.2
  86.7 2.0 collective-permute-start.11
  88.8 1.9 collective-permute-start.10
  90.8 4.8 %collective-permute-done.11 = f32[3,32,8,1]{3,2,1,0:T(8,128)S(1)} collective-permute-done((f32[3,32,8,1]{3,2,1,0:T(8,128)S(1)}, f32[3,32,8,1]{3,2,1,0:T(8,128)S(1)}, u32[]{:S(2)}, u32[]{:S(2)}) %collective-permute-start.11) | collective-permute-done | bytes 3104 | tf_op jit(solution)/shard_map/ppermute | solution.py:23
  95.6 7.6 %collective-permute-done.10 = f32[3,1,8,256]{3,2,1,0:T(8,128)S(1)} collective-permute-done((f32[3,1,8,256]{3,2,1,0:T(8,128)S(1)}, f32[3,1,8,256]{3,2,1,0:T(8,128)S(1)}, u32[]{:S(2)}, u32[]{:S(2)}) %collective-permute-start.10) | collective-permute-done | bytes 24608 | tf_op jit(solution)/shard_map/ppermute | solution.py:23
  103.2 0.4 maximum_subtract_fusion.9
  103.7 0.5 multiply_reduce_fusion
  104.3 0.6 fusion.1
  104.9 1.6 multiply_add_fusion
  106.6 0.8 slice.483
  107.4 1.3 collective-permute-start.13
  108.7 2.1 collective-permute-start.12
  110.8 1.6 select_reduce_fusion.7
  112.4 5.1 %maximum_add_fusion.2 = f32[4]{0:T(128)S(1)} fusion(f32[1]{0:T(128)} %bitcast.19, f32[1]{0:T(128)} %bitcast.18, f32[1]{0:T(128)} %bitcast.17, f32[1]{0:T(128)} %bitcast.16, f32[1]{0:T(128)} %bitcast.23, f32[1]{0:T(128)} %bitcast.22, f32[1]{0:T(128)} %bitcast.21, f32[1]{0:T(128)} %bitcast.20), kind=kLoop, calls=%fused_computation.132 | loop fusion | flops 28 | bytes 48 | tf_op jit(solution)/shard_map/add | solution.py:185
  117.5 1.1 pad_add_fusion
  118.7 76.3 %psum.16 = f32[4]{0:T(128)S(1)} all-reduce(f32[4]{0:T(128)S(1)} %maximum_add_fusion.2), channel_id=1, replica_groups=mesh['gy'=64,'gz'=4] {'gy','gz'}, use_global_device_ids=true, to_apply=%region_9.10 | all-reduce | flops 4 | bytes 32 | tf_op jit(solution)/shard_map/psum | solution.py:112
  194.9 0.3 slice.482
  195.4 1.3 maximum_subtract_fusion.11
  196.8 0.8 copy-done.8
  198.1 2.1 collective-permute-start.15
  200.2 1.9 collective-permute-start.14
  202.1 0.5 broadcast_multiply_fusion.7
  202.7 6.1 %collective-permute-done.15 = f32[3,32,8,1]{3,2,1,0:T(8,128)S(1)} collective-permute-done((f32[3,32,8,1]{3,2,1,0:T(8,128)S(1)}, f32[3,32,8,1]{3,2,1,0:T(8,128)S(1)}, u32[]{:S(2)}, u32[]{:S(2)}) %collective-permute-start.15) | collective-permute-done | bytes 3104 | tf_op jit(solution)/shard_map/ppermute | solution.py:23
  208.8 5.1 %collective-permute-done.14 = f32[3,1,8,256]{3,2,1,0:T(8,128)S(1)} collective-permute-done((f32[3,1,8,256]{3,2,1,0:T(8,128)S(1)}, f32[3,1,8,256]{3,2,1,0:T(8,128)S(1)}, u32[]{:S(2)}, u32[]{:S(2)}) %collective-permute-start.14) | collective-permute-done | bytes 24608 | tf_op jit(solution)/shard_map/ppermute | solution.py:23
  213.9 0.5 maximum_subtract_fusion.13
  214.5 1.1 fusion.9
  (98 shorter events, 4.6 us)
Async XLA Ops:
  0.6 2.3 %copy-start = (bf16[3,32,8,256]{3,2,1,0:T(8,128)(2,1)S(1)}, bf16[3,32,8,256]{3,2,1,0:T(8,128)(2,1)}, u32[]{:S(2)}) copy-start(bf16[3,32,8,256]{3,2,1,0:T(8,128)(2,1)} %param.15) | copy-start | bytes 1179652
  1.7 14.2 %collective-permute-start.1 = (f32[3,32,8,1]{3,2,1,0:T(8,128)S(1)}, f32[3,32,8,1]{3,2,1,0:T(8,128)S(1)}, u32[]{:S(2)}, u32[]{:S(2)}) collective-permute-start(f32[3,32,8,1]{3,2,1,0:T(8,128)S(1)} %slice.413), channel_id=1, source_target_pairs={{1,0},{2,1},{3,2},{5,4},{6,5},{7,6},{9,8},{10,9},{11,10},{13,12},{... | collective-permute-start | bytes 9224 | tf_op jit(solution)/shard_map/ppermute | solution.py:23
  3.0 11.0 %copy-start.20 = (f32[4]{0:T(128)S(1)}, f32[4]{0:T(128)}, u32[]{:S(2)}) copy-start(f32[4]{0:T(128)} %param.27) | copy-start | bytes 52
  3.0 12.8 %collective-permute-start = (f32[3,1,8,256]{3,2,1,0:T(8,128)S(1)}, f32[3,1,8,256]{3,2,1,0:T(8,128)S(1)}, u32[]{:S(2)}, u32[]{:S(2)}) collective-permute-start(f32[3,1,8,256]{3,2,1,0:T(8,128)S(1)} %slice.410), channel_id=1, source_target_pairs={{4,0},{8,4},{12,8},{16,12},{20,16},{24,20},{28,24},{32,28},{36,32}... | collective-permute-start | bytes 73736 | tf_op jit(solution)/shard_map/ppermute | solution.py:23
  14.8 1.0 copy-start.18
  16.1 1.0 copy-start.14
  17.2 9.6 %copy-start.13 = (s32[32,8,256]{2,1,0:T(8,128)S(1)}, s32[32,8,256]{2,1,0:T(8,128)}, u32[]{:S(2)}) copy-start(s32[32,8,256]{2,1,0:T(8,128)} %param.26) | copy-start | bytes 786436
  17.2 9.6 %copy-start.19 = (s32[32,8,256]{2,1,0:T(8,128)S(1)}, s32[32,8,256]{2,1,0:T(8,128)}, u32[]{:S(2)}) copy-start(s32[32,8,256]{2,1,0:T(8,128)} %param.25) | copy-start | bytes 786436
  17.4 13.0 %collective-permute-start.3 = (f32[3,32,8,1]{3,2,1,0:T(8,128)S(1)}, f32[3,32,8,1]{3,2,1,0:T(8,128)S(1)}, u32[]{:S(2)}, u32[]{:S(2)}) collective-permute-start(f32[3,32,8,1]{3,2,1,0:T(8,128)S(1)} %slice.423), channel_id=1, source_target_pairs={{0,1},{1,2},{2,3},{4,5},{5,6},{6,7},{8,9},{9,10},{10,11},{12,13},{... | collective-permute-start | bytes 9224 | tf_op jit(solution)/shard_map/ppermute | solution.py:23
  21.7 17.5 %collective-permute-start.2 = (f32[3,1,8,256]{3,2,1,0:T(8,128)S(1)}, f32[3,1,8,256]{3,2,1,0:T(8,128)S(1)}, u32[]{:S(2)}, u32[]{:S(2)}) collective-permute-start(f32[3,1,8,256]{3,2,1,0:T(8,128)S(1)} %slice.420), channel_id=1, source_target_pairs={{0,4},{4,8},{8,12},{12,16},{16,20},{20,24},{24,28},{28,32},{32,36}... | collective-permute-start | bytes 73736 | tf_op jit(solution)/shard_map/ppermute | solution.py:23
  39.6 1.0 copy-start.3
  39.6 1.1 copy-start.4
  41.1 1.0 copy-start.15
  42.4 3.4 %copy-start.5 = (f32[2,32,8,256]{3,2,1,0:T(8,128)S(1)}, f32[2,32,8,256]{3,2,1,0:T(8,128)}, u32[]{:S(2)}) copy-start(f32[2,32,8,256]{3,2,1,0:T(8,128)} %param.24) | copy-start | bytes 1572868
  42.5 9.8 %collective-permute-start.5 = (f32[3,32,8,1]{3,2,1,0:T(8,128)S(1)}, f32[3,32,8,1]{3,2,1,0:T(8,128)S(1)}, u32[]{:S(2)}, u32[]{:S(2)}) collective-permute-start(f32[3,32,8,1]{3,2,1,0:T(8,128)S(1)} %slice.437), channel_id=1, source_target_pairs={{1,0},{2,1},{3,2},{5,4},{6,5},{7,6},{9,8},{10,9},{11,10},{13,12},{... | collective-permute-start | bytes 9224 | tf_op jit(solution)/shard_map/ppermute | solution.py:23
  43.9 8.4 %collective-permute-start.4 = (f32[3,1,8,256]{3,2,1,0:T(8,128)S(1)}, f32[3,1,8,256]{3,2,1,0:T(8,128)S(1)}, u32[]{:S(2)}, u32[]{:S(2)}) collective-permute-start(f32[3,1,8,256]{3,2,1,0:T(8,128)S(1)} %slice.434), channel_id=1, source_target_pairs={{4,0},{8,4},{12,8},{16,12},{20,16},{24,20},{28,24},{32,28},{36,32}... | collective-permute-start | bytes 73736 | tf_op jit(solution)/shard_map/ppermute | solution.py:23
  53.0 9.7 %collective-permute-start.7 = (f32[3,32,8,1]{3,2,1,0:T(8,128)S(1)}, f32[3,32,8,1]{3,2,1,0:T(8,128)S(1)}, u32[]{:S(2)}, u32[]{:S(2)}) collective-permute-start(f32[3,32,8,1]{3,2,1,0:T(8,128)S(1)} %slice.447), channel_id=1, source_target_pairs={{0,1},{1,2},{2,3},{4,5},{5,6},{6,7},{8,9},{9,10},{10,11},{12,13},{... | collective-permute-start | bytes 9224 | tf_op jit(solution)/shard_map/ppermute | solution.py:23
  55.0 15.4 %collective-permute-start.6 = (f32[3,1,8,256]{3,2,1,0:T(8,128)S(1)}, f32[3,1,8,256]{3,2,1,0:T(8,128)S(1)}, u32[]{:S(2)}, u32[]{:S(2)}) collective-permute-start(f32[3,1,8,256]{3,2,1,0:T(8,128)S(1)} %slice.444), channel_id=1, source_target_pairs={{0,4},{4,8},{8,12},{12,16},{16,20},{20,24},{24,28},{28,32},{32,36}... | collective-permute-start | bytes 73736 | tf_op jit(solution)/shard_map/ppermute | solution.py:23
  71.6 1.1 copy-start.16
  73.2 1.1 copy-start.6
  73.2 1.4 copy-start.17
  73.3 1.3 copy-start.21
  75.1 9.7 %collective-permute-start.9 = (f32[3,32,8,1]{3,2,1,0:T(8,128)S(1)}, f32[3,32,8,1]{3,2,1,0:T(8,128)S(1)}, u32[]{:S(2)}, u32[]{:S(2)}) collective-permute-start(f32[3,32,8,1]{3,2,1,0:T(8,128)S(1)} %slice.461), channel_id=1, source_target_pairs={{1,0},{2,1},{3,2},{5,4},{6,5},{7,6},{9,8},{10,9},{11,10},{13,12},{... | collective-permute-start | bytes 9224 | tf_op jit(solution)/shard_map/ppermute | solution.py:23
  76.4 8.4 %collective-permute-start.8 = (f32[3,1,8,256]{3,2,1,0:T(8,128)S(1)}, f32[3,1,8,256]{3,2,1,0:T(8,128)S(1)}, u32[]{:S(2)}, u32[]{:S(2)}) collective-permute-start(f32[3,1,8,256]{3,2,1,0:T(8,128)S(1)} %slice.458), channel_id=1, source_target_pairs={{4,0},{8,4},{12,8},{16,12},{20,16},{24,20},{28,24},{32,28},{36,32}... | collective-permute-start | bytes 73736 | tf_op jit(solution)/shard_map/ppermute | solution.py:23
  78.4 0.7 copy-start.22
  85.1 1.3 copy-start.2
  85.3 17.9 %copy-start.7 = (f32[1,32,8,256]{3,2,1,0:T(8,128)}, f32[1,32,8,256]{3,2,1,0:T(8,128)S(1)}, u32[]{:S(2)}) copy-start(f32[1,32,8,256]{3,2,1,0:T(8,128)S(1)} %get-tuple-element.59) | copy-start | bytes 786436
  85.3 17.9 %copy-start.9 = (f32[1,32,8,256]{3,2,1,0:T(8,128)}, f32[1,32,8,256]{3,2,1,0:T(8,128)S(1)}, u32[]{:S(2)}) copy-start(f32[1,32,8,256]{3,2,1,0:T(8,128)S(1)} %get-tuple-element.60) | copy-start | bytes 786436
  85.3 17.9 %copy-start.11 = (f32[1,32,8,256]{3,2,1,0:T(8,128)}, f32[1,32,8,256]{3,2,1,0:T(8,128)S(1)}, u32[]{:S(2)}) copy-start(f32[1,32,8,256]{3,2,1,0:T(8,128)S(1)} %get-tuple-element.61) | copy-start | bytes 786436
  86.7 8.9 %collective-permute-start.11 = (f32[3,32,8,1]{3,2,1,0:T(8,128)S(1)}, f32[3,32,8,1]{3,2,1,0:T(8,128)S(1)}, u32[]{:S(2)}, u32[]{:S(2)}) collective-permute-start(f32[3,32,8,1]{3,2,1,0:T(8,128)S(1)} %slice.471), channel_id=1, source_target_pairs={{0,1},{1,2},{2,3},{4,5},{5,6},{6,7},{8,9},{9,10},{10,11},{12,13},{... | collective-permute-start | bytes 9224 | tf_op jit(solution)/shard_map/ppermute | solution.py:23
  88.8 14.5 %collective-permute-start.10 = (f32[3,1,8,256]{3,2,1,0:T(8,128)S(1)}, f32[3,1,8,256]{3,2,1,0:T(8,128)S(1)}, u32[]{:S(2)}, u32[]{:S(2)}) collective-permute-start(f32[3,1,8,256]{3,2,1,0:T(8,128)S(1)} %slice.468), channel_id=1, source_target_pairs={{0,4},{4,8},{8,12},{12,16},{16,20},{20,24},{24,28},{28,32},{32,36}... | collective-permute-start | bytes 73736 | tf_op jit(solution)/shard_map/ppermute | solution.py:23
  107.4 88.0 %collective-permute-start.13 = (f32[3,32,8,1]{3,2,1,0:T(8,128)}, f32[3,32,8,1]{3,2,1,0:T(8,128)}, u32[]{:S(2)}, u32[]{:S(2)}) collective-permute-start(f32[3,32,8,1]{3,2,1,0:T(8,128)} %slice.483), channel_id=1, source_target_pairs={{1,0},{2,1},{3,2},{5,4},{6,5},{7,6},{9,8},{10,9},{11,10},{13,12},{... | collective-permute-start | bytes 9224 | tf_op jit(solution)/shard_map/ppermute | solution.py:23
  108.7 86.7 %collective-permute-start.12 = (f32[3,1,8,256]{3,2,1,0:T(8,128)S(1)}, f32[3,1,8,256]{3,2,1,0:T(8,128)S(1)}, u32[]{:S(2)}, u32[]{:S(2)}) collective-permute-start(f32[3,1,8,256]{3,2,1,0:T(8,128)S(1)} %slice.480), channel_id=1, source_target_pairs={{4,0},{8,4},{12,8},{16,12},{20,16},{24,20},{28,24},{32,28},{36,32}... | collective-permute-start | bytes 73736 | tf_op jit(solution)/shard_map/ppermute | solution.py:23
  196.7 1.0 copy-start.8
  196.7 1.0 copy-start.10
  196.7 1.1 copy-start.12
  198.0 15.9 %copy-start.1 = (f32[3,32,8,256]{3,2,1,0:T(8,128)}, f32[3,32,8,256]{3,2,1,0:T(8,128)S(1)}, u32[]{:S(2)}) copy-start(f32[3,32,8,256]{3,2,1,0:T(8,128)S(1)} %maximum_add_fusion.1) | copy-start | bytes 2359300
  198.1 10.7 %collective-permute-start.15 = (f32[3,32,8,1]{3,2,1,0:T(8,128)S(1)}, f32[3,32,8,1]{3,2,1,0:T(8,128)S(1)}, u32[]{:S(2)}, u32[]{:S(2)}) collective-permute-start(f32[3,32,8,1]{3,2,1,0:T(8,128)S(1)} %slice.493), channel_id=1, source_target_pairs={{0,1},{1,2},{2,3},{4,5},{5,6},{6,7},{8,9},{9,10},{10,11},{12,13},{... | collective-permute-start | bytes 9224 | tf_op jit(solution)/shard_map/ppermute | solution.py:23
  200.2 13.7 %collective-permute-start.14 = (f32[3,1,8,256]{3,2,1,0:T(8,128)S(1)}, f32[3,1,8,256]{3,2,1,0:T(8,128)S(1)}, u32[]{:S(2)}, u32[]{:S(2)}) collective-permute-start(f32[3,1,8,256]{3,2,1,0:T(8,128)S(1)} %slice.490), channel_id=1, source_target_pairs={{0,4},{4,8},{8,12},{12,16},{16,20},{20,24},{24,28},{28,32},{32,36}... | collective-permute-start | bytes 73736 | tf_op jit(solution)/shard_map/ppermute | solution.py:23
where the time goes:
time: 217 us; the launch traced here: 216 us
  blocking collectives  76.3 us (35%)
  waiting for transfers between devices  56.5 us (26%)
  starting transfers between devices  43.4 us (20%)
  other arithmetic  23.4 us (11%)
  local copies, waits for them, and re-layouts  13.7 us (6%)
  between operations  2.27 us (1%)
    psum x1, blocking collectives, step_total(): return lax.psum(label_sums(material_labels, values, count), ('gy', 'gz'))  76.3 us
    ppermute x16, waiting for transfers between devices, shifted(): return lax.ppermute(block, axis, route)  56.5 us
    ppermute x16, starting transfers between devices, shifted(): return lax.ppermute(block, axis, route)  43.4 us
    unnamed x46, local copies, waits for them, and re-layouts  8.78 us
    add x1, other arithmetic, on_device(): step_total(material_labels, grad_second, count)  5.11 us
  transfers between devices with their start and end apart: 16, of which 9 were waited for; matrix products, arithmetic and copies ran while one was open for 7% of the time, Pallas kernels for 0%

commit v1 on v0

--- a/solution.py
+++ b/solution.py
@@ -109,7 +109,7 @@
 
 
 def step_total(material_labels, values, count):
-    return lax.psum(label_sums(material_labels, values, count), ("gy", "gz"))
+    return lax.psum(lax.psum(label_sums(material_labels, values, count), "gy"), "gz")
 
 
 def on_device(

time: 217 us -> 345 us (1.59)
  the two profiles are of different devices: /device:TPU:2 before, /device:TPU:32 now
where the time goes in v1:
time: 345 us; the launch traced here: 344 us
  blocking collectives  213 us (62%)
  starting transfers between devices  44.3 us (13%)
  waiting for transfers between devices  41.7 us (12%)
  other arithmetic  27.6 us (8%)
  local copies, waits for them, and re-layouts  14.7 us (4%)
    psum x1, blocking collectives, step_total(): lax.psum(label_sums(material_labels, values, count), 'gy')  203 us
    ppermute x16, starting transfers between devices, shifted(): return lax.ppermute(block, axis, route)  44.3 us
    ppermute x16, waiting for transfers between devices, shifted(): return lax.ppermute(block, axis, route)  41.7 us
    psum x1, blocking collectives, step_total(): lax.psum(lax.psum(label_sums(material_labels, values, count), 'gy'), 'gz')  10.2 us
    unnamed x68, local copies, waits for them, and re-layouts  9.8 us
  transfers between devices with their start and end apart: 16, of which 6 were waited for; matrix products, arithmetic and copies ran while one was open for 3% of the time, Pallas kernels for 0%

profile of v1, /device:TPU:32, one launch (start us, length us, event | category | flops | bytes accessed | tf_op | source)
XLA Modules:
  0.0 344.0 jit_solution(664427434805603892)
XLA Ops:
  0.6 1.0 slice.413
  1.7 3.7 %collective-permute-start.1 = (f32[3,32,8,1]{3,2,1,0:T(8,128)S(1)}, f32[3,32,8,1]{3,2,1,0:T(8,128)S(1)}, u32[]{:S(2)}, u32[]{:S(2)}) collective-permute-start(f32[3,32,8,1]{3,2,1,0:T(8,128)S(1)} %slice.413), channel_id=1, source_target_pairs={{1,0},{2,1},{3,2},{5,4},{6,5},{7,6},{9,8},{10,9},{11,10},{13,12},{... | collective-permute-start | bytes 9224 | tf_op jit(solution)/shard_map/ppermute | solution.py:23
  5.4 1.3 collective-permute-start
  6.7 0.6 fusion.15
  7.7 0.9 copy-done.29
  8.6 6.0 %collective-permute-done.1 = f32[3,32,8,1]{3,2,1,0:T(8,128)S(1)} collective-permute-done((f32[3,32,8,1]{3,2,1,0:T(8,128)S(1)}, f32[3,32,8,1]{3,2,1,0:T(8,128)S(1)}, u32[]{:S(2)}, u32[]{:S(2)}) %collective-permute-start.1) | collective-permute-done | bytes 3104 | tf_op jit(solution)/shard_map/ppermute | solution.py:23
  14.6 0.3 convert_subtract_fusion.2
  15.0 0.9 copy-done.14
  16.2 3.6 %collective-permute-start.3 = (f32[3,32,8,1]{3,2,1,0:T(8,128)S(1)}, f32[3,32,8,1]{3,2,1,0:T(8,128)S(1)}, u32[]{:S(2)}, u32[]{:S(2)}) collective-permute-start(f32[3,32,8,1]{3,2,1,0:T(8,128)S(1)} %slice.423), channel_id=1, source_target_pairs={{0,1},{1,2},{2,3},{4,5},{5,6},{6,7},{8,9},{9,10},{10,11},{12,13},{... | collective-permute-start | bytes 9224 | tf_op jit(solution)/shard_map/ppermute | solution.py:23
  19.8 5.4 %collective-permute-start.2 = (f32[3,1,8,256]{3,2,1,0:T(8,128)S(1)}, f32[3,1,8,256]{3,2,1,0:T(8,128)S(1)}, u32[]{:S(2)}, u32[]{:S(2)}) collective-permute-start(f32[3,1,8,256]{3,2,1,0:T(8,128)S(1)} %slice.420), channel_id=1, source_target_pairs={{0,4},{4,8},{8,12},{12,16},{16,20},{20,24},{24,28},{28,32},{32,36}... | collective-permute-start | bytes 73736 | tf_op jit(solution)/shard_map/ppermute | solution.py:23
  25.2 2.8 select_add_fusion.2
  28.8 0.4 maximum_subtract_fusion.1
  29.4 0.9 copy-done.3
  30.4 0.3 fusion.3
  30.8 0.9 copy-done.26
  31.7 0.3 multiply_reduce_fusion.3
  32.1 3.8 %collective-permute-start.5 = (f32[3,32,8,1]{3,2,1,0:T(8,128)S(1)}, f32[3,32,8,1]{3,2,1,0:T(8,128)S(1)}, u32[]{:S(2)}, u32[]{:S(2)}) collective-permute-start(f32[3,32,8,1]{3,2,1,0:T(8,128)S(1)} %slice.437), channel_id=1, source_target_pairs={{1,0},{2,1},{3,2},{5,4},{6,5},{7,6},{9,8},{10,9},{11,10},{13,12},{... | collective-permute-start | bytes 9224 | tf_op jit(solution)/shard_map/ppermute | solution.py:23
  35.9 1.3 collective-permute-start.4
  37.4 0.3 slice.436
  37.8 7.2 %collective-permute-done.5 = f32[3,32,8,1]{3,2,1,0:T(8,128)S(1)} collective-permute-done((f32[3,32,8,1]{3,2,1,0:T(8,128)S(1)}, f32[3,32,8,1]{3,2,1,0:T(8,128)S(1)}, u32[]{:S(2)}, u32[]{:S(2)}) %collective-permute-start.5) | collective-permute-done | bytes 3104 | tf_op jit(solution)/shard_map/ppermute | solution.py:23
  45.0 0.3 maximum_subtract_fusion.3
  45.8 4.4 %collective-permute-start.7 = (f32[3,32,8,1]{3,2,1,0:T(8,128)S(1)}, f32[3,32,8,1]{3,2,1,0:T(8,128)S(1)}, u32[]{:S(2)}, u32[]{:S(2)}) collective-permute-start(f32[3,32,8,1]{3,2,1,0:T(8,128)S(1)} %slice.447), channel_id=1, source_target_pairs={{0,1},{1,2},{2,3},{4,5},{5,6},{6,7},{8,9},{9,10},{10,11},{12,13},{... | collective-permute-start | bytes 9224 | tf_op jit(solution)/shard_map/ppermute | solution.py:23
  50.2 3.0 collective-permute-start.6
  53.5 5.9 %collective-permute-done.7 = f32[3,32,8,1]{3,2,1,0:T(8,128)S(1)} collective-permute-done((f32[3,32,8,1]{3,2,1,0:T(8,128)S(1)}, f32[3,32,8,1]{3,2,1,0:T(8,128)S(1)}, u32[]{:S(2)}, u32[]{:S(2)}) %collective-permute-start.7) | collective-permute-done | bytes 3104 | tf_op jit(solution)/shard_map/ppermute | solution.py:23
  59.4 0.4 maximum_subtract_fusion.5
  59.9 0.5 fusion.4
  60.6 1.0 copy-done.27
  61.6 0.5 multiply_reduce_fusion.1
  62.2 1.0 copy-done.6
  63.5 0.4 multiply_reduce_fusion.2
  64.0 1.9 collective-permute-start.9
  65.9 1.3 collective-permute-start.8
  67.3 0.6 copy-done.33
  68.2 1.1 negate_multiply_fusion.1
  69.3 0.3 slice.460
  69.7 8.3 %collective-permute-done.9 = f32[3,32,8,1]{3,2,1,0:T(8,128)S(1)} collective-permute-done((f32[3,32,8,1]{3,2,1,0:T(8,128)S(1)}, f32[3,32,8,1]{3,2,1,0:T(8,128)S(1)}, u32[]{:S(2)}, u32[]{:S(2)}) %collective-permute-start.9) | collective-permute-done | bytes 3104 | tf_op jit(solution)/shard_map/ppermute | solution.py:23
  78.0 0.3 maximum_subtract_fusion.7
  78.5 1.2 copy-done.2
  80.0 3.6 %collective-permute-start.11 = (f32[3,32,8,1]{3,2,1,0:T(8,128)S(1)}, f32[3,32,8,1]{3,2,1,0:T(8,128)S(1)}, u32[]{:S(2)}, u32[]{:S(2)}) collective-permute-start(f32[3,32,8,1]{3,2,1,0:T(8,128)S(1)} %slice.471), channel_id=1, source_target_pairs={{0,1},{1,2},{2,3},{4,5},{5,6},{6,7},{8,9},{9,10},{10,11},{12,13},{... | collective-permute-start | bytes 9224 | tf_op jit(solution)/shard_map/ppermute | solution.py:23
  83.6 3.0 collective-permute-start.10
  86.7 5.9 %collective-permute-done.11 = f32[3,32,8,1]{3,2,1,0:T(8,128)S(1)} collective-permute-done((f32[3,32,8,1]{3,2,1,0:T(8,128)S(1)}, f32[3,32,8,1]{3,2,1,0:T(8,128)S(1)}, u32[]{:S(2)}, u32[]{:S(2)}) %collective-permute-start.11) | collective-permute-done | bytes 3104 | tf_op jit(solution)/shard_map/ppermute | solution.py:23
  92.7 0.4 maximum_subtract_fusion.9
  93.2 0.4 multiply_reduce_fusion
  93.7 1.3 fusion.1
  95.0 1.6 multiply_add_fusion
  96.7 0.8 slice.483
  97.4 1.6 select_reduce_fusion.7
  99.0 5.1 %maximum_add_fusion.2 = f32[4]{0:T(128)S(1)} fusion(f32[1]{0:T(128)} %bitcast.19, f32[1]{0:T(128)} %bitcast.18, f32[1]{0:T(128)} %bitcast.17, f32[1]{0:T(128)} %bitcast.16, f32[1]{0:T(128)} %bitcast.23, f32[1]{0:T(128)} %bitcast.22, f32[1]{0:T(128)} %bitcast.21, f32[1]{0:T(128)} %bitcast.20), kind=kLoop, calls=%fused_computation.132 | loop fusion | flops 28 | bytes 48 | tf_op jit(solution)/shard_map/add | solution.py:185
  104.1 203.0 %psum.33 = f32[4]{0:T(128)S(1)} all-reduce(f32[4]{0:T(128)S(1)} %maximum_add_fusion.2), channel_id=1, replica_groups=mesh['gy'=64,'gz'=4] {'gy'}, use_global_device_ids=true, to_apply=%region_9.10 | all-reduce | flops 4 | bytes 32 | tf_op jit(solution)/shard_map/psum | solution.py:112
  307.1 1.2 negate_bitcast_fusion
  308.3 1.9 collective-permute-start.13
  310.2 1.3 collective-permute-start.12
  311.6 2.8 pad_add_fusion
  314.4 10.2 %psum.32 = f32[4]{0:T(128)S(1)} all-reduce(f32[4]{0:T(128)S(1)} %psum.33), channel_id=1, replica_groups=mesh['gy'=64,'gz'=4] {'gz'}, use_global_device_ids=true, to_apply=%region_10.11 | all-reduce | flops 4 | bytes 32 | tf_op jit(solution)/shard_map/psum | solution.py:112
  324.6 0.3 slice.482
  325.0 1.3 maximum_subtract_fusion.11
  326.4 0.8 copy-done.10
  327.7 3.4 collective-permute-start.15
  331.1 1.3 collective-permute-start.14
  332.4 0.5 broadcast_multiply_fusion.7
  332.9 8.4 %collective-permute-done.15 = f32[3,32,8,1]{3,2,1,0:T(8,128)S(1)} collective-permute-done((f32[3,32,8,1]{3,2,1,0:T(8,128)S(1)}, f32[3,32,8,1]{3,2,1,0:T(8,128)S(1)}, u32[]{:S(2)}, u32[]{:S(2)}) %collective-permute-start.15) | collective-permute-done | bytes 3104 | tf_op jit(solution)/shard_map/ppermute | solution.py:23
  341.3 0.5 maximum_subtract_fusion.13
  341.9 1.0 copy-done.8
  342.9 1.1 fusion.9
  (121 shorter events, 4.5 us)
Async XLA Ops:
  0.6 4.8 %copy-start = (bf16[3,32,8,256]{3,2,1,0:T(8,128)(2,1)S(1)}, bf16[3,32,8,256]{3,2,1,0:T(8,128)(2,1)}, u32[]{:S(2)}) copy-start(bf16[3,32,8,256]{3,2,1,0:T(8,128)(2,1)} %param.15) | copy-start | bytes 1179652
  1.7 12.9 %collective-permute-start.1 = (f32[3,32,8,1]{3,2,1,0:T(8,128)S(1)}, f32[3,32,8,1]{3,2,1,0:T(8,128)S(1)}, u32[]{:S(2)}, u32[]{:S(2)}) collective-permute-start(f32[3,32,8,1]{3,2,1,0:T(8,128)S(1)} %slice.413), channel_id=1, source_target_pairs={{1,0},{2,1},{3,2},{5,4},{6,5},{7,6},{9,8},{10,9},{11,10},{13,12},{... | collective-permute-start | bytes 9224 | tf_op jit(solution)/shard_map/ppermute | solution.py:23
  5.4 1.3 copy-start.31
  5.4 9.2 %collective-permute-start = (f32[3,1,8,256]{3,2,1,0:T(8,128)S(1)}, f32[3,1,8,256]{3,2,1,0:T(8,128)S(1)}, u32[]{:S(2)}, u32[]{:S(2)}) collective-permute-start(f32[3,1,8,256]{3,2,1,0:T(8,128)S(1)} %slice.410), channel_id=1, source_target_pairs={{4,0},{8,4},{12,8},{16,12},{20,16},{24,20},{28,24},{32,28},{36,32}... | collective-permute-start | bytes 73736 | tf_op jit(solution)/shard_map/ppermute | solution.py:23
  7.6 1.0 copy-start.29
  14.9 1.0 copy-start.14
  16.0 9.2 %copy-start.13 = (s32[32,8,256]{2,1,0:T(8,128)S(1)}, s32[32,8,256]{2,1,0:T(8,128)}, u32[]{:S(2)}) copy-start(s32[32,8,256]{2,1,0:T(8,128)} %param.26) | copy-start | bytes 786436
  16.0 9.2 %copy-start.30 = (s32[32,8,256]{2,1,0:T(8,128)S(1)}, s32[32,8,256]{2,1,0:T(8,128)}, u32[]{:S(2)}) copy-start(s32[32,8,256]{2,1,0:T(8,128)} %param.25) | copy-start | bytes 786436
  16.2 12.6 %collective-permute-start.3 = (f32[3,32,8,1]{3,2,1,0:T(8,128)S(1)}, f32[3,32,8,1]{3,2,1,0:T(8,128)S(1)}, u32[]{:S(2)}, u32[]{:S(2)}) collective-permute-start(f32[3,32,8,1]{3,2,1,0:T(8,128)S(1)} %slice.423), channel_id=1, source_target_pairs={{0,1},{1,2},{2,3},{4,5},{5,6},{6,7},{8,9},{9,10},{10,11},{12,13},{... | collective-permute-start | bytes 9224 | tf_op jit(solution)/shard_map/ppermute | solution.py:23
  19.8 9.0 %collective-permute-start.2 = (f32[3,1,8,256]{3,2,1,0:T(8,128)S(1)}, f32[3,1,8,256]{3,2,1,0:T(8,128)S(1)}, u32[]{:S(2)}, u32[]{:S(2)}) collective-permute-start(f32[3,1,8,256]{3,2,1,0:T(8,128)S(1)} %slice.420), channel_id=1, source_target_pairs={{0,4},{4,8},{8,12},{12,16},{16,20},{20,24},{24,28},{28,32},{32,36}... | collective-permute-start | bytes 73736 | tf_op jit(solution)/shard_map/ppermute | solution.py:23
  29.2 1.0 copy-start.3
  29.3 1.1 copy-start.4
  30.7 1.0 copy-start.26
  32.0 5.2 %copy-start.5 = (f32[2,32,8,256]{3,2,1,0:T(8,128)S(1)}, f32[2,32,8,256]{3,2,1,0:T(8,128)}, u32[]{:S(2)}) copy-start(f32[2,32,8,256]{3,2,1,0:T(8,128)} %param.24) | copy-start | bytes 1572868
  32.1 12.9 %collective-permute-start.5 = (f32[3,32,8,1]{3,2,1,0:T(8,128)S(1)}, f32[3,32,8,1]{3,2,1,0:T(8,128)S(1)}, u32[]{:S(2)}, u32[]{:S(2)}) collective-permute-start(f32[3,32,8,1]{3,2,1,0:T(8,128)S(1)} %slice.437), channel_id=1, source_target_pairs={{1,0},{2,1},{3,2},{5,4},{6,5},{7,6},{9,8},{10,9},{11,10},{13,12},{... | collective-permute-start | bytes 9224 | tf_op jit(solution)/shard_map/ppermute | solution.py:23
  35.9 9.1 %collective-permute-start.4 = (f32[3,1,8,256]{3,2,1,0:T(8,128)S(1)}, f32[3,1,8,256]{3,2,1,0:T(8,128)S(1)}, u32[]{:S(2)}, u32[]{:S(2)}) collective-permute-start(f32[3,1,8,256]{3,2,1,0:T(8,128)S(1)} %slice.434), channel_id=1, source_target_pairs={{4,0},{8,4},{12,8},{16,12},{20,16},{24,20},{28,24},{32,28},{36,32}... | collective-permute-start | bytes 73736 | tf_op jit(solution)/shard_map/ppermute | solution.py:23
  37.3 30.0 %copy-start.15 = (f32[1,32,8,256]{3,2,1,0:T(8,128)}, f32[1,32,8,256]{3,2,1,0:T(8,128)S(1)}, u32[]{:S(2)}) copy-start(f32[1,32,8,256]{3,2,1,0:T(8,128)S(1)} %get-tuple-element.91) | copy-start | bytes 786436
  37.3 30.0 %copy-start.17 = (f32[1,32,8,256]{3,2,1,0:T(8,128)}, f32[1,32,8,256]{3,2,1,0:T(8,128)S(1)}, u32[]{:S(2)}) copy-start(f32[1,32,8,256]{3,2,1,0:T(8,128)S(1)} %get-tuple-element.92) | copy-start | bytes 786436
  37.3 30.0 %copy-start.19 = (f32[1,32,8,256]{3,2,1,0:T(8,128)}, f32[1,32,8,256]{3,2,1,0:T(8,128)S(1)}, u32[]{:S(2)}) copy-start(f32[1,32,8,256]{3,2,1,0:T(8,128)S(1)} %get-tuple-element.93) | copy-start | bytes 786436
  37.3 30.0 %copy-start.21 = (f32[1,32,8,256]{3,2,1,0:T(8,128)}, f32[1,32,8,256]{3,2,1,0:T(8,128)S(1)}, u32[]{:S(2)}) copy-start(f32[1,32,8,256]{3,2,1,0:T(8,128)S(1)} %get-tuple-element.94) | copy-start | bytes 786436
  37.3 30.0 %copy-start.23 = (f32[1,32,8,256]{3,2,1,0:T(8,128)}, f32[1,32,8,256]{3,2,1,0:T(8,128)S(1)}, u32[]{:S(2)}) copy-start(f32[1,32,8,256]{3,2,1,0:T(8,128)S(1)} %get-tuple-element.95) | copy-start | bytes 786436
  45.8 13.6 %collective-permute-start.7 = (f32[3,32,8,1]{3,2,1,0:T(8,128)S(1)}, f32[3,32,8,1]{3,2,1,0:T(8,128)S(1)}, u32[]{:S(2)}, u32[]{:S(2)}) collective-permute-start(f32[3,32,8,1]{3,2,1,0:T(8,128)S(1)} %slice.447), channel_id=1, source_target_pairs={{0,1},{1,2},{2,3},{4,5},{5,6},{6,7},{8,9},{9,10},{10,11},{12,13},{... | collective-permute-start | bytes 9224 | tf_op jit(solution)/shard_map/ppermute | solution.py:23
  50.2 9.2 %collective-permute-start.6 = (f32[3,1,8,256]{3,2,1,0:T(8,128)S(1)}, f32[3,1,8,256]{3,2,1,0:T(8,128)S(1)}, u32[]{:S(2)}, u32[]{:S(2)}) collective-permute-start(f32[3,1,8,256]{3,2,1,0:T(8,128)S(1)} %slice.444), channel_id=1, source_target_pairs={{0,4},{4,8},{8,12},{12,16},{16,20},{20,24},{24,28},{28,32},{32,36}... | collective-permute-start | bytes 73736 | tf_op jit(solution)/shard_map/ppermute | solution.py:23
  60.5 1.1 copy-start.27
  62.1 1.1 copy-start.6
  62.1 1.4 copy-start.28
  62.2 1.3 copy-start.32
  64.0 14.0 %collective-permute-start.9 = (f32[3,32,8,1]{3,2,1,0:T(8,128)S(1)}, f32[3,32,8,1]{3,2,1,0:T(8,128)S(1)}, u32[]{:S(2)}, u32[]{:S(2)}) collective-permute-start(f32[3,32,8,1]{3,2,1,0:T(8,128)S(1)} %slice.461), channel_id=1, source_target_pairs={{1,0},{2,1},{3,2},{5,4},{6,5},{7,6},{9,8},{10,9},{11,10},{13,12},{... | collective-permute-start | bytes 9224 | tf_op jit(solution)/shard_map/ppermute | solution.py:23
  65.9 12.1 %collective-permute-start.8 = (f32[3,1,8,256]{3,2,1,0:T(8,128)S(1)}, f32[3,1,8,256]{3,2,1,0:T(8,128)S(1)}, u32[]{:S(2)}, u32[]{:S(2)}) collective-permute-start(f32[3,1,8,256]{3,2,1,0:T(8,128)S(1)} %slice.458), channel_id=1, source_target_pairs={{4,0},{8,4},{12,8},{16,12},{20,16},{24,20},{28,24},{32,28},{36,32}... | collective-permute-start | bytes 73736 | tf_op jit(solution)/shard_map/ppermute | solution.py:23
  67.2 0.9 copy-start.24
  67.2 0.9 copy-start.25
  67.3 0.7 copy-start.33
  78.3 1.3 copy-start.2
  78.5 14.2 %copy-start.9 = (f32[1,32,8,256]{3,2,1,0:T(8,128)}, f32[1,32,8,256]{3,2,1,0:T(8,128)S(1)}, u32[]{:S(2)}) copy-start(f32[1,32,8,256]{3,2,1,0:T(8,128)S(1)} %get-tuple-element.60) | copy-start | bytes 786436
  78.5 14.2 %copy-start.11 = (f32[1,32,8,256]{3,2,1,0:T(8,128)}, f32[1,32,8,256]{3,2,1,0:T(8,128)S(1)}, u32[]{:S(2)}) copy-start(f32[1,32,8,256]{3,2,1,0:T(8,128)S(1)} %get-tuple-element.61) | copy-start | bytes 786436
  80.0 12.7 %collective-permute-start.11 = (f32[3,32,8,1]{3,2,1,0:T(8,128)S(1)}, f32[3,32,8,1]{3,2,1,0:T(8,128)S(1)}, u32[]{:S(2)}, u32[]{:S(2)}) collective-permute-start(f32[3,32,8,1]{3,2,1,0:T(8,128)S(1)} %slice.471), channel_id=1, source_target_pairs={{0,1},{1,2},{2,3},{4,5},{5,6},{6,7},{8,9},{9,10},{10,11},{12,13},{... | collective-permute-start | bytes 9224 | tf_op jit(solution)/shard_map/ppermute | solution.py:23
  83.6 9.1 %collective-permute-start.10 = (f32[3,1,8,256]{3,2,1,0:T(8,128)S(1)}, f32[3,1,8,256]{3,2,1,0:T(8,128)S(1)}, u32[]{:S(2)}, u32[]{:S(2)}) collective-permute-start(f32[3,1,8,256]{3,2,1,0:T(8,128)S(1)} %slice.468), channel_id=1, source_target_pairs={{0,4},{4,8},{8,12},{12,16},{16,20},{20,24},{24,28},{28,32},{32,36}... | collective-permute-start | bytes 73736 | tf_op jit(solution)/shard_map/ppermute | solution.py:23
  95.0 1.6 copy-start.7
  307.1 4.4 %copy-start.16 = (f32[1,32,8,256]{3,2,1,0:T(8,128)S(1)}, f32[1,32,8,256]{3,2,1,0:T(8,128)}, u32[]{:S(2)}) copy-start(f32[1,32,8,256]{3,2,1,0:T(8,128)} %copy-done.15) | copy-start | bytes 786436
  307.1 4.4 %copy-start.18 = (f32[1,32,8,256]{3,2,1,0:T(8,128)S(1)}, f32[1,32,8,256]{3,2,1,0:T(8,128)}, u32[]{:S(2)}) copy-start(f32[1,32,8,256]{3,2,1,0:T(8,128)} %copy-done.17) | copy-start | bytes 786436
  307.1 4.4 %copy-start.20 = (f32[1,32,8,256]{3,2,1,0:T(8,128)S(1)}, f32[1,32,8,256]{3,2,1,0:T(8,128)}, u32[]{:S(2)}) copy-start(f32[1,32,8,256]{3,2,1,0:T(8,128)} %copy-done.19) | copy-start | bytes 786436
  307.1 4.4 %copy-start.22 = (f32[1,32,8,256]{3,2,1,0:T(8,128)S(1)}, f32[1,32,8,256]{3,2,1,0:T(8,128)}, u32[]{:S(2)}) copy-start(f32[1,32,8,256]{3,2,1,0:T(8,128)} %copy-done.21) | copy-start | bytes 786436
  308.3 16.7 %collective-permute-start.13 = (f32[3,32,8,1]{3,2,1,0:T(8,128)}, f32[3,32,8,1]{3,2,1,0:T(8,128)}, u32[]{:S(2)}, u32[]{:S(2)}) collective-permute-start(f32[3,32,8,1]{3,2,1,0:T(8,128)} %slice.483), channel_id=1, source_target_pairs={{1,0},{2,1},{3,2},{5,4},{6,5},{7,6},{9,8},{10,9},{11,10},{13,12},{... | collective-permute-start | bytes 9224 | tf_op jit(solution)/shard_map/ppermute | solution.py:23
  310.2 14.8 %collective-permute-start.12 = (f32[3,1,8,256]{3,2,1,0:T(8,128)S(1)}, f32[3,1,8,256]{3,2,1,0:T(8,128)S(1)}, u32[]{:S(2)}, u32[]{:S(2)}) collective-permute-start(f32[3,1,8,256]{3,2,1,0:T(8,128)S(1)} %slice.480), channel_id=1, source_target_pairs={{4,0},{8,4},{12,8},{16,12},{20,16},{24,20},{28,24},{32,28},{36,32}... | collective-permute-start | bytes 73736 | tf_op jit(solution)/shard_map/ppermute | solution.py:23
  326.3 1.0 copy-start.10
  326.3 1.0 copy-start.12
  327.5 13.8 %copy-start.1 = (f32[3,32,8,256]{3,2,1,0:T(8,128)}, f32[3,32,8,256]{3,2,1,0:T(8,128)S(1)}, u32[]{:S(2)}) copy-start(f32[3,32,8,256]{3,2,1,0:T(8,128)S(1)} %maximum_add_fusion.1) | copy-start | bytes 2359300
  327.7 13.6 %collective-permute-start.15 = (f32[3,32,8,1]{3,2,1,0:T(8,128)S(1)}, f32[3,32,8,1]{3,2,1,0:T(8,128)S(1)}, u32[]{:S(2)}, u32[]{:S(2)}) collective-permute-start(f32[3,32,8,1]{3,2,1,0:T(8,128)S(1)} %slice.493), channel_id=1, source_target_pairs={{0,1},{1,2},{2,3},{4,5},{5,6},{6,7},{8,9},{9,10},{10,11},{12,13},{... | collective-permute-start | bytes 9224 | tf_op jit(solution)/shard_map/ppermute | solution.py:23
  331.1 10.3 %collective-permute-start.14 = (f32[3,1,8,256]{3,2,1,0:T(8,128)S(1)}, f32[3,1,8,256]{3,2,1,0:T(8,128)S(1)}, u32[]{:S(2)}, u32[]{:S(2)}) collective-permute-start(f32[3,1,8,256]{3,2,1,0:T(8,128)S(1)} %slice.490), channel_id=1, source_target_pairs={{0,4},{4,8},{8,12},{12,16},{16,20},{20,24},{24,28},{28,32},{32,36}... | collective-permute-start | bytes 73736 | tf_op jit(solution)/shard_map/ppermute | solution.py:23
  341.8 1.1 copy-start.8
